TPU v7x, 32 devices: a whole 2x2x4 slice. The times are simulated.
32 devices in a mesh: groups: 2 (over y), zone: 4 (over x, core), tile: 4 (over z).
Axes of the slice: x: 2, y: 2, z: 4, core: 2. Of those that a mesh axis runs over, the one named last changes fastest.
Arguments:
- backscatter: bfloat16 [8, 2, 256, 512], P(('groups', 'zone'), None, 'tile'), parts along dimension 0, may hold values from -6 to 6
- row_bank: bfloat16 [16, 128, 128], replicated, may hold values from -0.3125 to 0.3125
- row_index: int32 [8, 4, 3], P(('groups', 'zone')), parts along dimension 0, may hold values from 0 to 3
- row_pick: int32 [8, 4, 3], P(('groups', 'zone')), parts along dimension 0, may hold values from 0 to 15
- row_mask: int32 [8, 4, 3], P(('groups', 'zone')), parts along dimension 0, may hold values 0 or 1
- column_bank: bfloat16 [16, 128, 128], replicated, may hold values from -0.3125 to 0.3125
- column_index: int32 [8, 2, 3], P(('groups', 'zone')), parts along dimension 0, may hold values from 0 to 1
- column_pick: int32 [8, 2, 3], P(('groups', 'zone')), parts along dimension 0, may hold values from 0 to 15
- column_mask: int32 [8, 2, 3], P(('groups', 'zone')), parts along dimension 0, may hold values 0 or 1
Outputs:
- geocoded: bfloat16 [8, 2, 256, 512], P(('groups', 'zone'), None, None, 'tile'), parts along dimension 0
There are 2 independent parts, one for each index of `groups`. A program takes and returns all parts, laid end to end along the dimension named above; an argument that names none is the same for every part. Nothing has to cross between parts.
All inputs are finite; a program needn't handle non-finite values. No bound on the sum of `row_mask` or of `column_mask` on one device may be relied on, other than what follows from the above.
Results may differ from a plain program's by a relative error of at most 0.0049.
Values may be sent and summed in bfloat16 or wider, within the bound.
No kernel may reach another device: no remote copies, remote signals or barrier semaphores. Data moves between devices by JAX's collectives and lax.ppermute only.
A program may use at most 64 MiB of HBM per device.

v0:
```python
import jax
import jax.numpy as jnp
from jax import lax
from jax.sharding import PartitionSpec as P

BLOCK = 128
EDGE = 64


def passed_along(block, axis, distance):
    devices = range(lax.axis_size(axis))
    route = [(i - distance, i) for i in devices if i - distance in devices]
    return lax.ppermute(block, axis, route)


def swap_panels(top_panel, bottom_panel):
    from_below = passed_along(top_panel, "zone", -1)
    from_above = passed_along(bottom_panel, "zone", 1)
    zone_index = lax.axis_index("zone")
    last_zone = lax.axis_size("zone") - 1
    feather = ((jnp.arange(EDGE, dtype=jnp.float32) + 0.5) / EDGE)[:, None]
    lower_blend = (
        (1.0 - feather) * bottom_panel.astype(jnp.float32)
        + feather * from_below.astype(jnp.float32)
    ).astype(jnp.bfloat16)
    upper_blend = (
        (1.0 - feather) * from_above.astype(jnp.float32) + feather * top_panel.astype(jnp.float32)
    ).astype(jnp.bfloat16)
    new_bottom = jnp.where(zone_index < last_zone, lower_blend, bottom_panel)
    new_top = jnp.where(zone_index > 0, upper_blend, top_panel)
    return (new_top, new_bottom)


def on_device(
    backscatter,
    row_bank,
    row_index,
    row_pick,
    row_mask,
    column_bank,
    column_index,
    column_pick,
    column_mask,
):
    image = backscatter[0]
    channels, lin_dev, samples = image.shape
    column_blocks = samples // BLOCK
    blocks = image.reshape(channels, lin_dev, column_blocks, BLOCK)
    gathered = blocks[:, :, row_index[0], :]
    row_weights = row_bank[row_pick[0]] * row_mask[0].astype(jnp.bfloat16)[:, :, None, None]
    along_samples = jnp.einsum(
        "clqbi,qbij->clqj", gathered, row_weights, preferred_element_type=jnp.float32
    )
    along_samples = along_samples.astype(jnp.bfloat16).reshape(channels, lin_dev, samples)
    line_blocks = column_index.shape[1]
    rows = line_blocks * BLOCK
    column_weights = (
        column_bank[column_pick[0]] * column_mask[0].astype(jnp.bfloat16)[:, :, None, None]
    )
    band_table = column_index[0]
    every_id = jnp.arange(line_blocks, dtype=jnp.int32)
    moved = lax.all_to_all(along_samples, "tile", split_axis=2, concat_axis=1, tiled=True)
    count = moved.shape[0]
    line_tiles = moved.reshape(count, line_blocks, BLOCK, BLOCK)
    picked = line_tiles[:, band_table[every_id]]
    result = jnp.einsum(
        "crbik,rboi->crok", picked, column_weights[every_id], preferred_element_type=jnp.float32
    )
    result = result.astype(jnp.bfloat16).reshape(count, every_id.shape[0] * BLOCK, BLOCK)
    new_top, new_bottom = swap_panels(result[:, :EDGE], result[:, rows - EDGE :])
    gridded = jnp.concatenate([new_top, result[:, EDGE : rows - EDGE], new_bottom], axis=1)
    return gridded[None]


def solution(mesh):
    in_specs = (
        P(("groups", "zone"), None, "tile", None),
        P(),
        P(("groups", "zone"), None, None),
        P(("groups", "zone"), None, None),
        P(("groups", "zone"), None, None),
        P(),
        P(("groups", "zone"), None, None),
        P(("groups", "zone"), None, None),
        P(("groups", "zone"), None, None),
    )
    out_specs = P(("groups", "zone"), None, None, "tile")
    return jax.shard_map(
        on_device, mesh=mesh, in_specs=in_specs, out_specs=out_specs, check_vma=False
    )
```

profile of v0, /device:TPU:1, one launch (start us, length us, event | category | flops | bytes accessed | tf_op | source)
XLA Modules:
  0.0 29.0 jit_solution(11059921443978826120)
XLA Ops:
  0.0 1.0 %reshape_squeeze.3 = bf16[2,64,4,128]{3,2,1,0:T(4,128)(2,1)S(1)} reshape(bf16[1,2,64,512]{3,2,1,0:T(8,128)(2,1)} %param.9) | data formatting | bytes 262144 | tf_op jit(solution)/shard_map/reshape;squeeze | solution.py:48
  1.0 0.6 %copy-done.2 = s32[1,4,3]{1,0,2:T(1,128)S(1)} copy-done((s32[1,4,3]{1,0,2:T(1,128)S(1)}, s32[1,4,3]{1,0,2:T(1,128)}, u32[]{:S(2)}) %copy-start.2) | copy-done | bytes 72
  1.9 0.7 %copy-done.3 = s32[1,4,3]{1,0,2:T(1,128)S(1)} copy-done((s32[1,4,3]{1,0,2:T(1,128)S(1)}, s32[1,4,3]{1,0,2:T(1,128)}, u32[]{:S(2)}) %copy-start.3) | copy-done | bytes 72
  2.8 0.7 %copy-done.4 = s32[1,4,3]{1,0,2:T(1,128)S(1)} copy-done((s32[1,4,3]{1,0,2:T(1,128)S(1)}, s32[1,4,3]{1,0,2:T(1,128)}, u32[]{:S(2)}) %copy-start.4) | copy-done | bytes 72
  3.5 0.6 %gather_fusion.3 = bf16[12,2,64,128]{3,2,1,0:T(8,128)(2,1)S(1)} fusion(bf16[2,64,4,128]{3,1,2,0:T(8,128)(2,1)S(1)} %copy.42, s32[1024]{0:T(1024)S(1)} %pad_clamp_fusion.1), kind=kCustom, calls=%fused_computation.3 | custom fusion | bytes 786480 | tf_op jit(solution)/shard_map/gather | solution.py:49
  4.2 0.6 %gather_fusion.2 = bf16[12,128,128]{2,1,0:T(8,128)(2,1)S(1)} fusion(bf16[16,128,128]{2,1,0:T(8,128)(2,1)S(1)} %copy-done, s32[1024]{0:T(1024)S(1)} %pad_clamp_fusion.2), kind=kCustom, calls=%fused_computation.2 | custom fusion | bytes 786480 | tf_op jit(solution)/shard_map/gather | solution.py:50
  4.8 0.3 %fusion.2 = bf16[2,64,4,128]{3,1,0,2:T(8,128)(2,1)S(1)} fusion(bf16[2,64,4,3,128]{4,1,0,3,2:T(8,128)(2,1)S(1)} %bitcast.85, bf16[4,3,128,128]{3,2,1,0:T(8,128)(2,1)S(1)} %bitcast.87, bf16[4,3]{1,0:T(4,128)(2,1)S(1)} %bitcast.89), kind=kOutput, calls=%fused_computation.10 | convolution fusion | flops 51183616 | bytes 917528 | tf_op jit(solution)/shard_map/clqbi,qbij->clqj/dot_general | solution.py:51
  5.2 0.2 copy.54
  5.3 0.9 %reshape.188 = bf16[4,2,8192]{2,1,0:T(2,128)(2,1)} reshape(bf16[512,2,64]{2,1,0:T(2,128)(2,1)S(1)} %bitcast.79) | data formatting | bytes 262144
  6.2 5.4 %all-to-all-start = ((bf16[4,2,8192]{2,1,0:T(2,128)(2,1)}), bf16[4,2,8192]{2,1,0:T(2,128)(2,1)S(1)}, u32[]{:S(2)}, u32[]{:S(2)}) async-start(bf16[4,2,8192]{2,1,0:T(2,128)(2,1)} %reshape.188), calls=%async_computation | async-start | bytes 262144 | tf_op jit(solution)/shard_map/all_to_all | solution.py:62
  11.7 0.7 %copy-done.5 = s32[1,2,3]{2,1,0:T(2,128)S(1)} copy-done((s32[1,2,3]{2,1,0:T(2,128)S(1)}, s32[1,2,3]{2,1,0:T(2,128)}, u32[]{:S(2)}) %copy-start.5) | copy-done | bytes 48
  12.4 0.7 %copy-done.6 = s32[1,2,3]{2,1,0:T(2,128)S(1)} copy-done((s32[1,2,3]{2,1,0:T(2,128)S(1)}, s32[1,2,3]{2,1,0:T(2,128)}, u32[]{:S(2)}) %copy-start.6) | copy-done | bytes 48
  13.1 0.7 %copy-done.1 = s32[1,2,3]{2,1,0:T(2,128)S(1)} copy-done((s32[1,2,3]{2,1,0:T(2,128)S(1)}, s32[1,2,3]{2,1,0:T(2,128)}, u32[]{:S(2)}) %copy-start.1) | copy-done | bytes 48
  13.8 0.6 %gather_fusion.4 = s32[2,3]{1,0:T(2,128)S(1)} fusion(s32[2,3]{1,0:T(2,128)S(1)} %bitcast.88, s32[1024]{0:T(1024)S(1)} %pad_clamp_fusion.3), kind=kCustom, calls=%fused_computation.4 | custom fusion | bytes 56 | tf_op jit(solution)/shard_map/gather | solution.py:65
  14.3 1.6 %gather_fusion = bf16[6,128,128]{2,1,0:T(8,128)(2,1)S(1)} fusion(bf16[16,128,128]{2,1,0:T(8,128)(2,1)} %param.14, s32[1024]{0:T(1024)S(1)} %pad_clamp_fusion.4), kind=kCustom, calls=%fused_computation | custom fusion | bytes 393240 | tf_op jit(solution)/shard_map/gather | solution.py:58
  16.1 0.6 %gather_fusion.1 = bf16[2,3,128,128]{3,2,1,0:T(8,128)(2,1)S(1)} fusion(bf16[2,3,128,128]{3,2,1,0:T(8,128)(2,1)S(1)} %broadcast_multiply_fusion, s32[1024]{0:T(1024)S(1)} %pad_clamp_fusion.3), kind=kCustom, calls=%fused_computation.1 | custom fusion | bytes 393224 | tf_op jit(solution)/shard_map/gather | solution.py:67
  16.8 0.2 reshape.189
  17.0 0.2 copy.55
  17.2 0.6 %gather_fusion.5 = bf16[6,2,128,128]{3,2,1,0:T(8,128)(2,1)S(1)} fusion(bf16[2,2,128,128]{3,2,1,0:T(8,128)(2,1)S(1)} %bitcast.77, s32[1024]{0:T(1024)S(1)} %pad_clamp_fusion), kind=kCustom, calls=%fused_computation.5 | custom fusion | bytes 786456 | tf_op jit(solution)/shard_map/gather | solution.py:65
  17.8 0.2 fusion.3
  18.1 4.9 %collective-permute-start = (bf16[2,64,128]{2,1,0:T(8,128)(2,1)S(1)}, bf16[2,64,128]{2,1,0:T(8,128)(2,1)S(1)}, u32[]{:S(2)}, u32[]{:S(2)}) collective-permute-start(bf16[2,64,128]{2,1,0:T(8,128)(2,1)S(1)} %get-tuple-element.7), channel_id=1, source_target_pairs={{0,4},{4,8},{8,12},{1,5},{5,9},{9,13},{2,6},{6,10},{10,14},{3,7},{... | collective-permute-start | bytes 98312 | tf_op jit(solution)/shard_map/ppermute | solution.py:13
  23.0 1.9 %collective-permute-start.1 = (bf16[2,64,128]{2,1,0:T(8,128)(2,1)S(1)}, bf16[2,64,128]{2,1,0:T(8,128)(2,1)S(1)}, u32[]{:S(2)}, u32[]{:S(2)}) collective-permute-start(bf16[2,64,128]{2,1,0:T(8,128)(2,1)S(1)} %get-tuple-element.8), channel_id=1, source_target_pairs={{4,0},{8,4},{12,8},{5,1},{9,5},{13,9},{6,2},{10,6},{14,10},{7,3},{... | collective-permute-start | bytes 98312 | tf_op jit(solution)/shard_map/ppermute | solution.py:13
  25.0 3.3 %collective-permute-done.1 = bf16[2,64,128]{2,1,0:T(8,128)(2,1)S(1)} collective-permute-done((bf16[2,64,128]{2,1,0:T(8,128)(2,1)S(1)}, bf16[2,64,128]{2,1,0:T(8,128)(2,1)S(1)}, u32[]{:S(2)}, u32[]{:S(2)}) %collective-permute-start.1) | collective-permute-done | bytes 32800 | tf_op jit(solution)/shard_map/ppermute | solution.py:13
  28.3 0.7 %maximum_bitcast_fusion = bf16[1,2,256,128]{3,2,1,0:T(8,128)(2,1)} fusion(bf16[2,64,128]{2,1,0:T(8,128)(2,1)S(1)} %get-tuple-element.6, bf16[2,128,128]{2,1,0:T(8,128)(2,1)S(1)} %slice.26, bf16[2,64,128]{2,1,0:T(8,128)(2,1)S(1)} %get-tuple-element.5), kind=kLoop, calls=%fused_computation.16 | loop fusion | flops 393216 | bytes 262144 | tf_op jit(solution)/shard_map/broadcast_in_dim | solution.py:72
  (37 shorter events, 1.0 us)
Async XLA Ops:
  0.0 4.2 %copy-start = (bf16[16,128,128]{2,1,0:T(8,128)(2,1)S(1)}, bf16[16,128,128]{2,1,0:T(8,128)(2,1)}, u32[]{:S(2)}) copy-start(bf16[16,128,128]{2,1,0:T(8,128)(2,1)} %param.10) | copy-start | bytes 1572868
  1.0 0.7 %copy-start.2 = (s32[1,4,3]{1,0,2:T(1,128)S(1)}, s32[1,4,3]{1,0,2:T(1,128)}, u32[]{:S(2)}) copy-start(s32[1,4,3]{1,0,2:T(1,128)} %param.11) | copy-start | bytes 148
  1.9 0.7 %copy-start.3 = (s32[1,4,3]{1,0,2:T(1,128)S(1)}, s32[1,4,3]{1,0,2:T(1,128)}, u32[]{:S(2)}) copy-start(s32[1,4,3]{1,0,2:T(1,128)} %param.12) | copy-start | bytes 148
  2.7 0.7 %copy-start.4 = (s32[1,4,3]{1,0,2:T(1,128)S(1)}, s32[1,4,3]{1,0,2:T(1,128)}, u32[]{:S(2)}) copy-start(s32[1,4,3]{1,0,2:T(1,128)} %param.13) | copy-start | bytes 148
  6.2 10.5 %all-to-all-start = ((bf16[4,2,8192]{2,1,0:T(2,128)(2,1)}), bf16[4,2,8192]{2,1,0:T(2,128)(2,1)S(1)}, u32[]{:S(2)}, u32[]{:S(2)}) async-start(bf16[4,2,8192]{2,1,0:T(2,128)(2,1)} %reshape.188), calls=%async_computation | async-start | bytes 262144 | tf_op jit(solution)/shard_map/all_to_all | solution.py:62
  11.6 0.7 %copy-start.5 = (s32[1,2,3]{2,1,0:T(2,128)S(1)}, s32[1,2,3]{2,1,0:T(2,128)}, u32[]{:S(2)}) copy-start(s32[1,2,3]{2,1,0:T(2,128)} %param.16) | copy-start | bytes 76
  12.4 0.7 %copy-start.6 = (s32[1,2,3]{2,1,0:T(2,128)S(1)}, s32[1,2,3]{2,1,0:T(2,128)}, u32[]{:S(2)}) copy-start(s32[1,2,3]{2,1,0:T(2,128)} %param.17) | copy-start | bytes 76
  13.1 0.7 %copy-start.1 = (s32[1,2,3]{2,1,0:T(2,128)S(1)}, s32[1,2,3]{2,1,0:T(2,128)}, u32[]{:S(2)}) copy-start(s32[1,2,3]{2,1,0:T(2,128)} %param.15) | copy-start | bytes 76
  18.1 6.9 %collective-permute-start = (bf16[2,64,128]{2,1,0:T(8,128)(2,1)S(1)}, bf16[2,64,128]{2,1,0:T(8,128)(2,1)S(1)}, u32[]{:S(2)}, u32[]{:S(2)}) collective-permute-start(bf16[2,64,128]{2,1,0:T(8,128)(2,1)S(1)} %get-tuple-element.7), channel_id=1, source_target_pairs={{0,4},{4,8},{8,12},{1,5},{5,9},{9,13},{2,6},{6,10},{10,14},{3,7},{... | collective-permute-start | bytes 98312 | tf_op jit(solution)/shard_map/ppermute | solution.py:13
  23.0 5.2 %collective-permute-start.1 = (bf16[2,64,128]{2,1,0:T(8,128)(2,1)S(1)}, bf16[2,64,128]{2,1,0:T(8,128)(2,1)S(1)}, u32[]{:S(2)}, u32[]{:S(2)}) collective-permute-start(bf16[2,64,128]{2,1,0:T(8,128)(2,1)S(1)} %get-tuple-element.8), channel_id=1, source_target_pairs={{4,0},{8,4},{12,8},{5,1},{9,5},{13,9},{6,2},{10,6},{14,10},{7,3},{... | collective-permute-start | bytes 98312 | tf_op jit(solution)/shard_map/ppermute | solution.py:13
where the time goes:
time: 29.4 us; the launch traced here: 29 us
  starting transfers between devices  12.2 us (41%)
  local copies, waits for them, and re-layouts  11.8 us (40%)
  waiting for transfers between devices  3.26 us (11%)
  other arithmetic  0.91 us (3%)
  matrix products  0.57 us (2%)
    ppermute x2, starting transfers between devices, passed_along(): return lax.ppermute(block, axis, route)  6.83 us
    all_to_all x1, starting transfers between devices, on_device(): lax.all_to_all(along_samples, 'tile', split_axis=2, concat_axis=1, tiled=...  5.41 us
    unnamed x16, local copies, waits for them, and re-layouts  5.14 us
    ppermute x2, waiting for transfers between devices, passed_along(): return lax.ppermute(block, axis, route)  3.26 us
    gather x1, local copies, waits for them, and re-layouts, on_device(): column_bank[column_pick[0]]  1.62 us
    gather x2, local copies, waits for them, and re-layouts, on_device(): picked = line_tiles[:, band_table[every_id]]  1.18 us
    another operation x2, local copies, waits for them, and re-layouts, on_device(): blocks = image.reshape(channels, lin_dev, column_blocks, BLOCK)  1.02 us
    broadcast_in_dim x1, other arithmetic, on_device(): return gridded[None]  0.67 us
  transfers between devices with their start and end apart: 3, of which 1 were waited for; matrix products, arithmetic and copies ran while one was open for 11% of the time, Pallas kernels for 0%

commit v1 on v0

--- a/solution.py
+++ b/solution.py
@@ -59,7 +59,29 @@
     )
     band_table = column_index[0]
     every_id = jnp.arange(line_blocks, dtype=jnp.int32)
-    moved = lax.all_to_all(along_samples, "tile", split_axis=2, concat_axis=1, tiled=True)
+
+    def limits_spread(u_in, dev_axis):
+        inter = lax.axis_index(dev_axis)
+        val = lax.axis_size(dev_axis)
+        n_now, formed = (val, inter)
+        e_now = list(u_in.shape)
+        lower = u_in.shape[2] // n_now
+        e_now[2] = lower
+        b_next = e_now[1]
+        e_now[1] = b_next * n_now
+        block_out = jnp.zeros(e_now, u_in.dtype)
+        for at in range(n_now):
+            answer = lax.dynamic_slice_in_dim(u_in, (formed ^ at) * lower, lower, axis=2)
+            if at:
+                answer = lax.ppermute(
+                    answer, axis_name=dev_axis, perm=[(rr, rr ^ at) for rr in range(n_now)]
+                )
+            block_out = lax.dynamic_update_slice_in_dim(
+                block_out, answer, (formed ^ at) * b_next, axis=1
+            )
+        return block_out
+
+    moved = limits_spread(along_samples, "tile")
     count = moved.shape[0]
     line_tiles = moved.reshape(count, line_blocks, BLOCK, BLOCK)
     picked = line_tiles[:, band_table[every_id]]

time: 29.4 us -> 26.3 us (0.89)
  local copies, waits for them, and re-layouts: 11.8 us -> 9.24 us
  starting transfers between devices: 12.2 us -> 11.7 us
    all_to_all x1 -> x0, starting transfers between devices: 5.41 us -> none  [on_device(): lax.all_to_all(along_samples, 'tile', split_axis=2, concat_axis=1, tiled=...]
    ppermute x0 -> x3, starting transfers between devices: none -> 4.49 us  [limits_spread(): lax.ppermute(answer, axis_name=dev_axis, perm=[(rr, rr ^ at) for rr in ra...]
    unnamed x16 -> x14, local copies, waits for them, and re-layouts: 5.14 us -> 2.8 us
    ppermute x2, starting transfers between devices: 6.83 us -> 7.2 us  [passed_along(): return lax.ppermute(block, axis, route)]
  transfers between devices with their start and end apart: 3 -> 5, of which waited for: 1 -> 1; matrix products, arithmetic and copies ran while one was open for 11% -> 12% of each run, Pallas kernels for 0% -> 0%
where the time goes in v1:
time: 26.3 us; the launch traced here: 26 us
  starting transfers between devices  11.7 us (44%)
  local copies, waits for them, and re-layouts  9.24 us (35%)
  waiting for transfers between devices  3.28 us (12%)
  other arithmetic  0.91 us (3%)
  matrix products  0.56 us (2%)
  between operations  0.29 us (1%)
    ppermute x2, starting transfers between devices, passed_along(): return lax.ppermute(block, axis, route)  7.2 us
    ppermute x3, starting transfers between devices, limits_spread(): lax.ppermute(answer, axis_name=dev_axis, perm=[(rr, rr ^ at) for rr in ra...  4.49 us
    ppermute x2, waiting for transfers between devices, passed_along(): return lax.ppermute(block, axis, route)  3.26 us
    unnamed x14, local copies, waits for them, and re-layouts  2.8 us
    gather x1, local copies, waits for them, and re-layouts, on_device(): column_bank[column_pick[0]]  1.62 us
    gather x2, local copies, waits for them, and re-layouts, on_device(): picked = line_tiles[:, band_table[every_id]]  1.18 us
    another operation x2, local copies, waits for them, and re-layouts, on_device(): blocks = image.reshape(channels, lin_dev, column_blocks, BLOCK)  1.02 us
    broadcast_in_dim x1, other arithmetic, on_device(): return gridded[None]  0.67 us
  transfers between devices with their start and end apart: 5, of which 1 were waited for; matrix products, arithmetic and copies ran while one was open for 12% of the time, Pallas kernels for 0%

profile of v1, /device:TPU:1, one launch (start us, length us, event | category | flops | bytes accessed | tf_op | source)
XLA Modules:
  0.0 26.0 jit_solution(1329208109903131483)
XLA Ops:
  0.0 1.0 %reshape_squeeze.3 = bf16[2,64,4,128]{3,2,1,0:T(4,128)(2,1)S(1)} reshape(bf16[1,2,64,512]{3,2,1,0:T(8,128)(2,1)} %param.9) | data formatting | bytes 262144 | tf_op jit(solution)/shard_map/reshape;squeeze | solution.py:48
  1.1 0.6 %copy-done.3 = s32[1,4,3]{1,0,2:T(1,128)S(1)} copy-done((s32[1,4,3]{1,0,2:T(1,128)S(1)}, s32[1,4,3]{1,0,2:T(1,128)}, u32[]{:S(2)}) %copy-start.3) | copy-done | bytes 72
  1.7 0.1 copy.22
  1.9 0.1 copy.20
  2.1 0.7 %copy-done.2 = s32[1,4,3]{1,0,2:T(1,128)S(1)} copy-done((s32[1,4,3]{1,0,2:T(1,128)S(1)}, s32[1,4,3]{1,0,2:T(1,128)}, u32[]{:S(2)}) %copy-start.2) | copy-done | bytes 72
  2.8 0.1 copy.21
  2.9 0.6 %gather_fusion.3 = bf16[12,2,64,128]{3,2,1,0:T(8,128)(2,1)S(1)} fusion(bf16[2,64,4,128]{3,1,2,0:T(8,128)(2,1)S(1)} %copy.23, s32[1024]{0:T(1024)S(1)} %pad_clamp_fusion.1), kind=kCustom, calls=%fused_computation.3 | custom fusion | bytes 786480 | tf_op jit(solution)/shard_map/gather | solution.py:49
  3.5 0.6 %gather_fusion.2 = bf16[12,128,128]{2,1,0:T(8,128)(2,1)S(1)} fusion(bf16[16,128,128]{2,1,0:T(8,128)(2,1)S(1)} %copy-done, s32[1024]{0:T(1024)S(1)} %pad_clamp_fusion.2), kind=kCustom, calls=%fused_computation.2 | custom fusion | bytes 786480 | tf_op jit(solution)/shard_map/gather | solution.py:50
  4.1 0.3 %fusion.2 = bf16[4,2,8,8,128]{4,3,2,1,0:T(8,128)(2,1)S(1)} fusion(bf16[2,64,4,3,128]{4,1,0,3,2:T(8,128)(2,1)S(1)} %bitcast.82, bf16[4,3,128,128]{3,2,1,0:T(8,128)(2,1)S(1)} %bitcast.84, bf16[4,3]{1,0:T(4,128)(2,1)S(1)} %bitcast.86), kind=kOutput, calls=%fused_computation.10 | convolution fusion | flops 51183616 | bytes 917528 | tf_op jit(solution)/shard_map/clqbi,qbij->clqj/dot_general | solution.py:51
  4.6 2.2 %collective-permute-start = (bf16[2,64,128]{2,1,0:T(8,128)(2,1)S(1)}, bf16[2,64,128]{2,1,0:T(8,128)(2,1)S(1)}, u32[]{:S(2)}, u32[]{:S(2)}) collective-permute-start(bf16[2,64,128]{2,1,0:T(8,128)(2,1)S(1)} %get-tuple-element.11), channel_id=1, source_target_pairs={{0,1},{1,0},{2,3},{3,2},{4,5},{5,4},{6,7},{7,6},{8,9},{9,8},{10,11... | collective-permute-start | bytes 98312 | tf_op jit(solution)/shard_map/ppermute | solution.py:76
  6.8 2.3 %collective-permute-start.1 = (bf16[2,64,128]{2,1,0:T(8,128)(2,1)S(1)}, bf16[2,64,128]{2,1,0:T(8,128)(2,1)S(1)}, u32[]{:S(2)}, u32[]{:S(2)}) collective-permute-start(bf16[2,64,128]{2,1,0:T(8,128)(2,1)S(1)} %get-tuple-element.10), channel_id=1, source_target_pairs={{0,2},{1,3},{2,0},{3,1},{4,6},{5,7},{6,4},{7,5},{8,10},{9,11},{10,... | collective-permute-start | bytes 98312 | tf_op jit(solution)/shard_map/ppermute | solution.py:76
  9.1 0.7 %copy-done.1 = s32[1,2,3]{2,1,0:T(2,128)S(1)} copy-done((s32[1,2,3]{2,1,0:T(2,128)S(1)}, s32[1,2,3]{2,1,0:T(2,128)}, u32[]{:S(2)}) %copy-start.1) | copy-done | bytes 48
  9.8 0.6 %gather_fusion.4 = s32[2,3]{1,0:T(2,128)S(1)} fusion(s32[2,3]{1,0:T(2,128)S(1)} %bitcast.85, s32[1024]{0:T(1024)S(1)} %pad_clamp_fusion.3), kind=kCustom, calls=%fused_computation.4 | custom fusion | bytes 56 | tf_op jit(solution)/shard_map/gather | solution.py:87
  10.4 0.1 copy-done.5
  10.7 0.7 %copy-done.6 = s32[1,2,3]{2,1,0:T(2,128)S(1)} copy-done((s32[1,2,3]{2,1,0:T(2,128)S(1)}, s32[1,2,3]{2,1,0:T(2,128)}, u32[]{:S(2)}) %copy-start.6) | copy-done | bytes 48
  11.3 1.6 %gather_fusion = bf16[6,128,128]{2,1,0:T(8,128)(2,1)S(1)} fusion(bf16[16,128,128]{2,1,0:T(8,128)(2,1)} %param.14, s32[1024]{0:T(1024)S(1)} %pad_clamp_fusion.4), kind=kCustom, calls=%fused_computation | custom fusion | bytes 393240 | tf_op jit(solution)/shard_map/gather | solution.py:58
  13.1 0.6 %gather_fusion.1 = bf16[2,3,128,128]{3,2,1,0:T(8,128)(2,1)S(1)} fusion(bf16[2,3,128,128]{3,2,1,0:T(8,128)(2,1)S(1)} %broadcast_multiply_fusion, s32[1024]{0:T(1024)S(1)} %pad_clamp_fusion.3), kind=kCustom, calls=%fused_computation.1 | custom fusion | bytes 393224 | tf_op jit(solution)/shard_map/gather | solution.py:89
  13.8 0.6 %gather_fusion.5 = bf16[6,2,128,128]{3,2,1,0:T(8,128)(2,1)S(1)} fusion(bf16[2,2,128,128]{3,2,1,0:T(8,128)(2,1)S(1)} %bitcast.76, s32[1024]{0:T(1024)S(1)} %pad_clamp_fusion), kind=kCustom, calls=%fused_computation.5 | custom fusion | bytes 786456 | tf_op jit(solution)/shard_map/gather | solution.py:87
  14.4 0.2 fusion.3
  14.7 5.3 %collective-permute-start.3 = (bf16[2,64,128]{2,1,0:T(8,128)(2,1)S(1)}, bf16[2,64,128]{2,1,0:T(8,128)(2,1)S(1)}, u32[]{:S(2)}, u32[]{:S(2)}) collective-permute-start(bf16[2,64,128]{2,1,0:T(8,128)(2,1)S(1)} %get-tuple-element.7), channel_id=1, source_target_pairs={{0,4},{4,8},{8,12},{1,5},{5,9},{9,13},{2,6},{6,10},{10,14},{3,7},{... | collective-permute-start | bytes 98312 | tf_op jit(solution)/shard_map/ppermute | solution.py:13
  20.0 1.9 %collective-permute-start.4 = (bf16[2,64,128]{2,1,0:T(8,128)(2,1)S(1)}, bf16[2,64,128]{2,1,0:T(8,128)(2,1)S(1)}, u32[]{:S(2)}, u32[]{:S(2)}) collective-permute-start(bf16[2,64,128]{2,1,0:T(8,128)(2,1)S(1)} %get-tuple-element.8), channel_id=1, source_target_pairs={{4,0},{8,4},{12,8},{5,1},{9,5},{13,9},{6,2},{10,6},{14,10},{7,3},{... | collective-permute-start | bytes 98312 | tf_op jit(solution)/shard_map/ppermute | solution.py:13
  21.9 3.3 %collective-permute-done.4 = bf16[2,64,128]{2,1,0:T(8,128)(2,1)S(1)} collective-permute-done((bf16[2,64,128]{2,1,0:T(8,128)(2,1)S(1)}, bf16[2,64,128]{2,1,0:T(8,128)(2,1)S(1)}, u32[]{:S(2)}, u32[]{:S(2)}) %collective-permute-start.4) | collective-permute-done | bytes 32800 | tf_op jit(solution)/shard_map/ppermute | solution.py:13
  25.2 0.1 fusion.8
  25.3 0.7 %maximum_bitcast_fusion = bf16[1,2,256,128]{3,2,1,0:T(8,128)(2,1)} fusion(bf16[2,64,128]{2,1,0:T(8,128)(2,1)S(1)} %get-tuple-element.6, bf16[2,128,128]{2,1,0:T(8,128)(2,1)S(1)} %slice.26, bf16[2,64,128]{2,1,0:T(8,128)(2,1)S(1)} %get-tuple-element.5), kind=kLoop, calls=%fused_computation.17 | loop fusion | flops 393216 | bytes 262144 | tf_op jit(solution)/shard_map/broadcast_in_dim | solution.py:94
  (40 shorter events, 0.7 us)
Async XLA Ops:
  0.0 3.5 %copy-start = (bf16[16,128,128]{2,1,0:T(8,128)(2,1)S(1)}, bf16[16,128,128]{2,1,0:T(8,128)(2,1)}, u32[]{:S(2)}) copy-start(bf16[16,128,128]{2,1,0:T(8,128)(2,1)} %param.10) | copy-start | bytes 1572868
  1.0 0.7 %copy-start.3 = (s32[1,4,3]{1,0,2:T(1,128)S(1)}, s32[1,4,3]{1,0,2:T(1,128)}, u32[]{:S(2)}) copy-start(s32[1,4,3]{1,0,2:T(1,128)} %param.11) | copy-start | bytes 148
  1.0 0.7 %copy-start.4 = (s32[1,4,3]{1,0,2:T(1,128)S(1)}, s32[1,4,3]{1,0,2:T(1,128)}, u32[]{:S(2)}) copy-start(s32[1,4,3]{1,0,2:T(1,128)} %param.12) | copy-start | bytes 148
  2.1 0.7 %copy-start.2 = (s32[1,4,3]{1,0,2:T(1,128)S(1)}, s32[1,4,3]{1,0,2:T(1,128)}, u32[]{:S(2)}) copy-start(s32[1,4,3]{1,0,2:T(1,128)} %param.13) | copy-start | bytes 148
  4.6 9.1 %collective-permute-start = (bf16[2,64,128]{2,1,0:T(8,128)(2,1)S(1)}, bf16[2,64,128]{2,1,0:T(8,128)(2,1)S(1)}, u32[]{:S(2)}, u32[]{:S(2)}) collective-permute-start(bf16[2,64,128]{2,1,0:T(8,128)(2,1)S(1)} %get-tuple-element.11), channel_id=1, source_target_pairs={{0,1},{1,0},{2,3},{3,2},{4,5},{5,4},{6,7},{7,6},{8,9},{9,8},{10,11... | collective-permute-start | bytes 98312 | tf_op jit(solution)/shard_map/ppermute | solution.py:76
  6.8 6.9 %collective-permute-start.1 = (bf16[2,64,128]{2,1,0:T(8,128)(2,1)S(1)}, bf16[2,64,128]{2,1,0:T(8,128)(2,1)S(1)}, u32[]{:S(2)}, u32[]{:S(2)}) collective-permute-start(bf16[2,64,128]{2,1,0:T(8,128)(2,1)S(1)} %get-tuple-element.10), channel_id=1, source_target_pairs={{0,2},{1,3},{2,0},{3,1},{4,6},{5,7},{6,4},{7,5},{8,10},{9,11},{10,... | collective-permute-start | bytes 98312 | tf_op jit(solution)/shard_map/ppermute | solution.py:76
  9.1 4.7 %collective-permute-start.2 = (bf16[2,64,128]{2,1,0:T(8,128)(2,1)S(1)}, bf16[2,64,128]{2,1,0:T(8,128)(2,1)S(1)}, u32[]{:S(2)}, u32[]{:S(2)}) collective-permute-start(bf16[2,64,128]{2,1,0:T(8,128)(2,1)S(1)} %get-tuple-element.9), channel_id=1, source_target_pairs={{0,3},{1,2},{2,1},{3,0},{4,7},{5,6},{6,5},{7,4},{8,11},{9,10},{10,... | collective-permute-start | bytes 98312 | tf_op jit(solution)/shard_map/ppermute | solution.py:76
  9.1 0.7 %copy-start.1 = (s32[1,2,3]{2,1,0:T(2,128)S(1)}, s32[1,2,3]{2,1,0:T(2,128)}, u32[]{:S(2)}) copy-start(s32[1,2,3]{2,1,0:T(2,128)} %param.15) | copy-start | bytes 76
  9.8 0.7 %copy-start.5 = (s32[1,2,3]{2,1,0:T(2,128)S(1)}, s32[1,2,3]{2,1,0:T(2,128)}, u32[]{:S(2)}) copy-start(s32[1,2,3]{2,1,0:T(2,128)} %param.16) | copy-start | bytes 76
  10.7 0.7 %copy-start.6 = (s32[1,2,3]{2,1,0:T(2,128)S(1)}, s32[1,2,3]{2,1,0:T(2,128)}, u32[]{:S(2)}) copy-start(s32[1,2,3]{2,1,0:T(2,128)} %param.17) | copy-start | bytes 76
  14.7 7.2 %collective-permute-start.3 = (bf16[2,64,128]{2,1,0:T(8,128)(2,1)S(1)}, bf16[2,64,128]{2,1,0:T(8,128)(2,1)S(1)}, u32[]{:S(2)}, u32[]{:S(2)}) collective-permute-start(bf16[2,64,128]{2,1,0:T(8,128)(2,1)S(1)} %get-tuple-element.7), channel_id=1, source_target_pairs={{0,4},{4,8},{8,12},{1,5},{5,9},{9,13},{2,6},{6,10},{10,14},{3,7},{... | collective-permute-start | bytes 98312 | tf_op jit(solution)/shard_map/ppermute | solution.py:13
  20.0 5.2 %collective-permute-start.4 = (bf16[2,64,128]{2,1,0:T(8,128)(2,1)S(1)}, bf16[2,64,128]{2,1,0:T(8,128)(2,1)S(1)}, u32[]{:S(2)}, u32[]{:S(2)}) collective-permute-start(bf16[2,64,128]{2,1,0:T(8,128)(2,1)S(1)} %get-tuple-element.8), channel_id=1, source_target_pairs={{4,0},{8,4},{12,8},{5,1},{9,5},{13,9},{6,2},{10,6},{14,10},{7,3},{... | collective-permute-start | bytes 98312 | tf_op jit(solution)/shard_map/ppermute | solution.py:13
